TPU v7x, 32 devices: a whole 2x2x4 slice. The times are simulated.
32 devices in a mesh: seq: 8 (over z, x), exp: 4 (over y, core).
Axes of the slice: x: 2, y: 2, z: 4, core: 2. Of those that a mesh axis runs over, the one named last changes fastest.
Arguments:
- queries: bfloat16 [1024, 4096], P('seq', 'exp'), may hold values from -2 to 2
- keys: bfloat16 [1024, 4096], P('seq', 'exp'), may hold values from -2 to 2
- values: bfloat16 [1024, 4096], P('seq', 'exp'), may hold values from -6 to 6
- log_decay: float32 [1024, 32], P('seq', 'exp'), may hold values from -1 to 0, as said below
- residual: bfloat16 [1024, 4096], P(('seq', 'exp')), may hold values from -6 to 6
- attn_gain: float32 [4096], replicated, may hold values from 0.25 to 1.75
- moe_gain: float32 [4096], replicated, may hold values from 0.25 to 1.75
- expert_ids: int32 [1024, 2], P(('seq', 'exp')), may hold values from 0 to 3, all different within a row; in each aligned block of 32 rows (0 to 31, 32 to 63, ...) at most 24 rows name the same one
- gate_weights: float32 [1024, 2], P(('seq', 'exp')), may hold values from 0.2 to 1
- w_gate: bfloat16 [4, 9216, 4096], P('exp', 'seq'), may hold values from -0.09375 to 0.09375
- w_up: bfloat16 [4, 9216, 4096], P('exp', 'seq'), may hold values from -0.09375 to 0.09375
- w_down: bfloat16 [4, 9216, 4096], P('exp', 'seq'), may hold values from -0.0625 to 0.0625
Outputs:
- layer_out: bfloat16 [1024, 4096], P(('seq', 'exp'))
Inputs may be any that keep to these rules, and one draw needn't show every extreme that they name: `expert_ids`: each token names two different experts. In each aligned block of 32 tokens (the tokens of one device) no expert is named by more than 24 tokens, a bound that some block reaches. `log_decay`: every entry is negative.
All inputs are finite; a program needn't handle non-finite values.
Results may differ from a plain program's by a relative error of at most 0.012.
Values may be sent and summed in bfloat16 or wider, within the bound.
A program may use at most 128 MiB of HBM per device.

v0:
```python
import jax
import jax.numpy as jnp
from jax import lax
from jax.sharding import PartitionSpec as P


def carried_in(value, axis, join, neutral):
    place = lax.axis_index(axis)
    gathered = jax.tree.map(
        lambda a, kind: lax.all_gather(a.astype(kind), axis), value, (jnp.bfloat16, jnp.bfloat16)
    )
    state = jax.tree.map(lambda a, e: jnp.zeros_like(a) + jnp.asarray(e, a.dtype), value, neutral)

    def one(hop, state):
        return join(
            state,
            jax.tree.map(
                lambda a, own: lax.dynamic_index_in_dim(a, hop, 0, False).astype(own.dtype),
                gathered,
                value,
            ),
        )

    return lax.fori_loop(0, place, one, state)


def combine_states(earlier, later):
    return (earlier[0] + later[0], jnp.exp(later[0])[:, None, None] * earlier[1] + later[1])


def route_targets(ids_block, experts, capacity):
    flat_ids = ids_block.reshape(-1)
    onehot = (flat_ids[:, None] == jnp.arange(experts, dtype=jnp.int32)[None, :]).astype(jnp.int32)
    before = jnp.cumsum(onehot, axis=0) - onehot
    slot_index = jnp.sum(before * onehot, axis=1)
    return flat_ids * capacity + slot_index


def body(
    queries,
    keys,
    values,
    log_decay,
    residual,
    attn_gain,
    moe_gain,
    expert_ids,
    gate_weights,
    w_gate,
    w_up,
    w_down,
):
    rows = queries.shape[0]
    heads = log_decay.shape[1]
    head_dim = queries.shape[1] // heads
    q_heads = queries.reshape(rows, heads, head_dim)
    k_heads = keys.reshape(rows, heads, head_dim)
    v_heads = values.reshape(rows, heads, head_dim)
    log_cum = jnp.cumsum(log_decay, axis=0)
    block_total = log_cum[-1]
    keys_weighted = (k_heads * jnp.exp(block_total[None, :] - log_cum)[:, :, None]).astype(
        jnp.bfloat16
    )
    block_state = jnp.einsum(
        "thd,the->hde", keys_weighted, v_heads, preferred_element_type=jnp.float32
    )
    identity_pair = (
        jnp.zeros((heads,), jnp.float32),
        jnp.zeros((heads, head_dim, head_dim), jnp.float32),
    )
    carried = carried_in((block_total, block_state), "seq", combine_states, identity_pair)[1]
    scores = jnp.einsum("thd,shd->hts", q_heads, k_heads, preferred_element_type=jnp.float32)
    gap_logs = log_cum.T[:, :, None] - log_cum.T[:, None, :]
    causal_mask = (
        lax.broadcasted_iota(jnp.int32, (rows, rows), 0)
        >= lax.broadcasted_iota(jnp.int32, (rows, rows), 1)
    )[None, :, :]
    weights = jnp.where(
        causal_mask, scores * jnp.exp(jnp.where(causal_mask, gap_logs, 0.0)), 0.0
    ).astype(jnp.bfloat16)
    intra = jnp.einsum("hts,she->the", weights, v_heads, preferred_element_type=jnp.float32)
    inter = jnp.exp(log_cum)[:, :, None] * jnp.einsum(
        "thd,hde->the", q_heads.astype(jnp.float32), carried, precision=lax.Precision.HIGHEST
    )
    attn = intra + inter
    normed = (attn * lax.rsqrt(jnp.mean(attn * attn, axis=-1, keepdims=True) + 1e-06)).astype(
        jnp.bfloat16
    )
    normed = normed.reshape(rows, heads * head_dim)
    token_major = lax.all_to_all(normed, "exp", split_axis=0, concat_axis=1, tiled=True)
    hidden = (residual.astype(jnp.float32) + token_major.astype(jnp.float32) * attn_gain).astype(
        jnp.bfloat16
    )
    hid32 = hidden.astype(jnp.float32)
    moe_in = (
        hid32 * lax.rsqrt(jnp.mean(hid32 * hid32, axis=-1, keepdims=True) + 1e-06) * moe_gain
    ).astype(jnp.bfloat16)
    exp_count = lax.axis_size("exp")
    tok_rows = residual.shape[0]
    width = residual.shape[1]
    local_experts = w_gate.shape[0]
    experts = local_experts * exp_count
    capacity = max(2, (3 * tok_rows + experts - 1) // experts)
    slots = experts * capacity
    slot_range = jnp.arange(slots, dtype=jnp.int32)
    target = route_targets(expert_ids, experts, capacity)
    selector = (target[None, :] == slot_range[:, None]).astype(jnp.bfloat16)
    doubled = jnp.repeat(moe_in, 2, axis=0)
    outgoing = jnp.dot(selector, doubled, preferred_element_type=jnp.float32).astype(jnp.bfloat16)
    outgoing = outgoing.reshape(exp_count, local_experts, capacity, width)
    arrived = lax.all_to_all(outgoing, "exp", split_axis=0, concat_axis=0, tiled=True)
    piece = lax.all_gather(arrived, "seq", axis=0, tiled=True)
    gate_part = jnp.einsum("ajcd,jfd->ajcf", piece, w_gate, preferred_element_type=jnp.float32)
    up_part = jnp.einsum("ajcd,jfd->ajcf", piece, w_up, preferred_element_type=jnp.float32)
    active = (jax.nn.silu(gate_part) * up_part).astype(jnp.bfloat16)
    piece = active
    summed = lax.psum_scatter(
        jnp.einsum("ajcf,jfd->ajcd", piece, w_down, preferred_element_type=jnp.float32).astype(
            jnp.bfloat16
        ),
        "seq",
        scatter_dimension=0,
        tiled=True,
    )
    returned = lax.all_to_all(summed, "exp", split_axis=0, concat_axis=0, tiled=True)
    flat_back = returned.reshape(slots, width)
    picked = lax.dot_general(
        selector, flat_back, (((0,), (0,)), ((), ())), preferred_element_type=jnp.float32
    )
    picked = picked.reshape(tok_rows, 2, width)
    mixed = hid32 + jnp.sum(gate_weights[:, :, None] * picked, axis=1)
    return mixed.astype(jnp.bfloat16)


def solution(mesh):
    in_specs = (
        P("seq", "exp"),
        P("seq", "exp"),
        P("seq", "exp"),
        P("seq", "exp"),
        P(("seq", "exp"), None),
        P(),
        P(),
        P(("seq", "exp"), None),
        P(("seq", "exp"), None),
        P("exp", "seq", None),
        P("exp", "seq", None),
        P("exp", "seq", None),
    )
    out_specs = P(("seq", "exp"), None)
    return jax.shard_map(body, mesh=mesh, in_specs=in_specs, out_specs=out_specs, check_vma=False)
```

profile of v0, /device:TPU:0, one launch (start us, length us, event | category | flops | bytes accessed | tf_op | source)
XLA Modules:
  0.0 371.7 jit_solution(4224046115400613152)
XLA Ops:
  6.5 0.0 copy-start
  6.5 0.0 copy-start.1
  6.5 0.0 all-gather.7.cloned.1.call-start
  6.5 0.8 copy.83
  7.4 0.2 reduce_window_sum.22
  7.6 1.1 copy.101
  8.8 0.0 copy-done
  8.8 0.9 convolution_convert_fusion.1
  9.7 0.0 all-gather.7.cloned.1.call-update
  9.8 22.3 %all-gather.1 = bf16[8,1,8]{2,1,0:T(2,128)(2,1)S(1)} all-gather(bf16[1,1,8]{2,1,0:T(2,128)(2,1)S(1)} %convert_bitcast_fusion.1), channel_id=1, replica_groups=mesh['seq'=8,'exp'=4] {'seq'}, dimensions={0}, use_global_device_ids=true | all-gather | bytes 144 | tf_op jit(solution)/shard_map/all_gather | solution.py:10
  32.1 0.1 copy.84
  32.2 0.8 copy.95
  33.0 0.1 reshape.137
  33.1 0.1 fusion.66
  33.1 0.1 reduce_window_sum.23
  33.3 0.2 select_reduce_fusion
  33.5 28.3 %all-gather.7.cloned.1.call-done = bf16[64,128,128]{2,1,0:T(8,128)(2,1)} async-done(((bf16[8,128,128]{2,1,0:T(8,128)(2,1)}), bf16[64,128,128]{2,1,0:T(8,128)(2,1)}) %all-gather.7.cloned.1.call-update) | async-done | bytes 2097168 | tf_op jit(solution)/shard_map/all_gather | solution.py:10
  61.8 0.0 copy-start.2
  61.8 0.0 copy-start.3
  61.8 0.0 copy-start.4
  61.8 0.0 copy-done.1
  61.8 0.6 fusion.42
  62.4 0.5 multiply_reduce_fusion
  63.0 0.2 copy.93
  63.2 0.8 all_to_all.16
  64.0 3.4 all-to-all-start
  67.4 0.0 all-gather.5.cloned.1.call-start
  67.5 5.9 %all-to-all-done = bf16[4,32,1024]{2,1,0:T(8,128)(2,1)S(1)} async-done(((bf16[4,32,1024]{2,1,0:T(8,128)(2,1)}), bf16[4,32,1024]{2,1,0:T(8,128)(2,1)S(1)}, u32[]{:S(2)}, u32[]{:S(2)}) %all-to-all-start) | async-done | bytes 262176 | tf_op jit(solution)/shard_map/all_to_all | solution.py:90
  73.5 0.0 copy-done.2
  73.5 0.0 copy-done.3
  73.5 0.2 fusion.44
  73.7 0.0 copy-done.4
  73.7 0.1 fusion.46
  73.9 0.5 broadcast_in_dim.24
  74.4 0.2 reshape.138
  74.6 0.3 convolution_convert_fusion
  74.9 14.7 %all_to_all.23 = bf16[4,1,24,4096]{3,2,1,0:T(8,128)(2,1)} all-to-all(bf16[4,1,24,4096]{3,2,1,0:T(8,128)(2,1)S(1)} %bitcast.144), channel_id=1, replica_groups=mesh['seq'=8,'exp'=4] {'exp'}, dimensions={0} | all-to-all | bytes 1572864 | tf_op jit(solution)/shard_map/all_to_all | solution.py:111
  89.7 0.0 all-gather.5.cloned.1.call-update
  89.7 0.2 reduce-scatter.2.cloned.1.call-start
  89.9 104.3 %all-gather.5.cloned.1.call-done = bf16[32,1,24,4096]{3,2,1,0:T(8,128)(2,1)} async-done(((bf16[4,1,24,4096]{3,2,1,0:T(8,128)(2,1)}), bf16[32,1,24,4096]{3,2,1,0:T(8,128)(2,1)}) %all-gather.5.cloned.1.call-update) | async-done | bytes 6291472 | tf_op jit(solution)/shard_map/all_gather | solution.py:112
  194.2 0.0 slice-start
  194.2 0.0 slice-start.1
  194.3 12.0 %fusion.14 = f32[32,1,24,1152]{3,2,0,1:T(8,128)S(1)} fusion(bf16[1,1152,4096]{2,1,0:T(8,128)(2,1)} %param.23, bf16[32,1,24,4096]{3,2,1,0:T(8,128)(2,1)} %all-gather.5.cloned.1.call-done), kind=kOutput, calls=%fused_computation.14 | convolution fusion | flops 7247757312 | bytes 19267584 | tf_op jit(solution)/shard_map/ajcd,jfd->ajcf/dot_general | solution.py:113
  206.3 0.0 slice-start.2
  206.3 14.5 %fusion.34 = bf16[32,24,1152]{2,1,0:T(8,128)(2,1)} fusion(bf16[1,1152,4096]{2,1,0:T(8,128)(2,1)} %param.24, bf16[32,1,24,4096]{3,2,1,0:T(8,128)(2,1)} %all-gather.5.cloned.1.call-done, f32[32,1,24,1152]{3,2,0,1:T(8,128)S(1)} %fusion.14), kind=kOutput, calls=%fused_computation.18 | convolution fusion | flops 7253065728 | bytes 21037056 | tf_op jit(solution)/shard_map/ajcd,jfd->ajcf/dot_general | solution.py:114
  220.8 0.0 slice-done
  220.8 0.0 slice-done.1
  220.8 0.0 slice-done.2
  220.8 11.7 %fusion.11 = bf16[32,1,24,4096]{3,2,0,1:T(8,128)(2,1)} fusion(bf16[32,24,1152]{2,1,0:T(8,128)(2,1)} %fusion.34, bf16[1,1152,4096]{2,1,0:T(8,128)(2,1)S(1)} %bitcast.153), kind=kOutput, calls=%fused_computation.11 | convolution fusion | flops 7250903040 | bytes 17498112 | tf_op jit(solution)/shard_map/ajcf,jfd->ajcd/dot_general | solution.py:118
  232.5 0.0 copy-start.5
  232.5 0.0 copy-start.6
  232.6 0.0 reduce-scatter.2.cloned.1.call-update
  232.6 116.4 %reduce-scatter.2.cloned.1.call-done = bf16[4,1,24,4096]{3,2,0,1:T(8,128)(2,1)} async-done(((bf16[32,1,24,4096]{3,2,0,1:T(8,128)(2,1)}), bf16[4,1,24,4096]{3,2,0,1:T(8,128)(2,1)}) %reduce-scatter.2.cloned.1.call-update) | async-done | bytes 786448 | tf_op jit(solution)/shard_map/reduce_scatter | solution.py:117
  349.0 3.5 all-to-all-start.2
  352.5 0.1 reduce_sum.40
  352.6 0.1 copy.96
  352.7 0.0 copy-done.5
  352.7 11.4 %all-to-all-done.2 = bf16[4,1,24,4096]{3,2,1,0:T(8,128)(2,1)S(1)} async-done(((bf16[4,1,24,4096]{3,2,1,0:T(8,128)(2,1)}), bf16[4,1,24,4096]{3,2,1,0:T(8,128)(2,1)S(1)}, u32[]{:S(2)}, u32[]{:S(2)}) %all-to-all-start.2) | async-done | bytes 786464 | tf_op jit(solution)/shard_map/all_to_all | solution.py:125
  364.1 0.0 copy-done.6
  364.1 0.3 fusion.39
  364.4 0.8 fusion.47
  (17 shorter events, 0.4 us)
Async XLA Ops:
  6.5 2.3 copy-start
  6.5 55.3 %copy-start.1 = (bf16[128,1024]{1,0:T(8,128)(2,1)S(1)}, bf16[128,1024]{1,0:T(8,128)(2,1)}, u32[]{:S(2)}) copy-start(bf16[128,1024]{1,0:T(8,128)(2,1)} %param.14) | copy-start | bytes 786436
  6.5 55.2 %all-gather.7.cloned.1.call-start = ((), (), s32[]{:S(2)}) async-start(), calls=%async_computation.6 | async-start | bytes 2359296 | tf_op jit(solution)/shard_map/all_gather | solution.py:10
  61.8 11.7 %copy-start.2 = (bf16[32,4096]{1,0:T(8,128)(2,1)S(1)}, bf16[32,4096]{1,0:T(8,128)(2,1)}, u32[]{:S(2)}) copy-start(bf16[32,4096]{1,0:T(8,128)(2,1)} %param.18) | copy-start | bytes 786436
  61.8 11.7 %copy-start.3 = (f32[4096]{0:T(1024)S(1)}, f32[4096]{0:T(1024)}, u32[]{:S(2)}) copy-start(f32[4096]{0:T(1024)} %param.19) | copy-start | bytes 49156
  61.8 12.0 %copy-start.4 = (f32[4096]{0:T(1024)S(1)}, f32[4096]{0:T(1024)}, u32[]{:S(2)}) copy-start(f32[4096]{0:T(1024)} %param.20) | copy-start | bytes 49156
  64.0 9.4 %all-to-all-start = ((bf16[4,32,1024]{2,1,0:T(8,128)(2,1)}), bf16[4,32,1024]{2,1,0:T(8,128)(2,1)S(1)}, u32[]{:S(2)}, u32[]{:S(2)}) async-start(bf16[4,32,1024]{2,1,0:T(8,128)(2,1)} %all_to_all.16), calls=%async_computation | async-start | bytes 524288 | tf_op jit(solution)/shard_map/all_to_all | solution.py:90
  67.4 126.8 %all-gather.5.cloned.1.call-start = ((), (), s32[]{:S(2)}) async-start(), calls=%async_computation.4 | async-start | bytes 7077888 | tf_op jit(solution)/shard_map/all_gather | solution.py:112
  89.7 259.3 %reduce-scatter.2.cloned.1.call-start = ((), (), s32[]{:S(2)}) async-start(), calls=%async_computation.5 | async-start | bytes 7077888 | tf_op jit(solution)/shard_map/reduce_scatter | solution.py:117
  194.2 26.5 %slice-start = ((s8[9437184]{0:T(1024)(128)(4,1)}), s8[4194304]{0:T(1024)(128)(4,1)S(1)}, s32[]{:S(2)}) async-start(s8[9437184]{0:T(1024)(128)(4,1)} %bitcast.152), calls=%async_computation.7 | async-start | bytes 8388608
  194.2 26.5 %slice-start.1 = ((s8[9437184]{0:T(1024)(128)(4,1)}), s8[4194304]{0:T(1024)(128)(4,1)S(1)}, s32[]{:S(2)}) async-start(s8[9437184]{0:T(1024)(128)(4,1)} %bitcast.152), calls=%async_computation.8 | async-start | bytes 8388608
  206.3 14.5 %slice-start.2 = ((s8[9437184]{0:T(1024)(128)(4,1)}), s8[1048576]{0:T(1024)(128)(4,1)S(1)}, s32[]{:S(2)}) async-start(s8[9437184]{0:T(1024)(128)(4,1)} %bitcast.152), calls=%async_computation.9 | async-start | bytes 2097152
  232.5 120.1 %copy-start.5 = (s32[32,2]{0,1:T(2,128)S(1)}, s32[32,2]{0,1:T(2,128)}, u32[]{:S(2)}) copy-start(s32[32,2]{0,1:T(2,128)} %param.21) | copy-start | bytes 772
  232.5 131.5 %copy-start.6 = (f32[32,2]{0,1:T(2,128)S(1)}, f32[32,2]{0,1:T(2,128)}, u32[]{:S(2)}) copy-start(f32[32,2]{0,1:T(2,128)} %param.22) | copy-start | bytes 772
  349.0 15.1 %all-to-all-start.2 = ((bf16[4,1,24,4096]{3,2,1,0:T(8,128)(2,1)}), bf16[4,1,24,4096]{3,2,1,0:T(8,128)(2,1)S(1)}, u32[]{:S(2)}, u32[]{:S(2)}) async-start(bf16[4,1,24,4096]{3,2,1,0:T(8,128)(2,1)} %bitcast.149), calls=%async_computation.3 | async-start | bytes 1572864 | tf_op jit(solution)/shard_map/all_to_all | solution.py:125
Sparse Core Ops, SparseCore 0:
  9.9 51.7 all-gather.6
  89.8 104.4 all-gather.4
  232.7 116.2 reduce-scatter.1
where the time goes:
time: 372 us
  waiting for transfers between devices  266 us (72%)
  matrix products  41 us (11%)
  blocking collectives  37 us (10%)
  between operations  13.4 us (4%)
  starting transfers between devices  7.17 us (2%)
  local copies, waits for them, and re-layouts  5.01 us (1%)
    reduce_scatter x1, waiting for transfers between devices, body(): lax.psum_scatter(jnp.einsum('ajcf,jfd->ajcd', piece, w_down, preferred_el...  116 us
    all_gather x1, waiting for transfers between devices, body(): piece = lax.all_gather(arrived, 'seq', axis=0, tiled=True)  104 us
    all_gather x1, waiting for transfers between devices, carried_in(): lax.all_gather(a.astype(kind), axis)  28.3 us
    all_gather x1, blocking collectives, carried_in(): lax.all_gather(a.astype(kind), axis)  22.3 us
    all_to_all x1, blocking collectives, body(): lax.all_to_all(outgoing, 'exp', split_axis=0, concat_axis=0, tiled=True)  14.7 us
    dot_general x1, matrix products, body(): jnp.einsum('ajcd,jfd->ajcf', piece, w_up, preferred_element_type=jnp.floa...  14.5 us
    dot_general x1, matrix products, body(): jnp.einsum('ajcd,jfd->ajcf', piece, w_gate, preferred_element_type=jnp.fl...  12 us
    dot_general x1, matrix products, body(): jnp.einsum('ajcf,jfd->ajcd', piece, w_down, preferred_element_type=jnp.fl...  11.7 us
  transfers between devices with their start and end apart: 5, of which 5 were waited for; matrix products, arithmetic and copies ran while one was open for 0% of the time, Pallas kernels for 0%

commit v1 on v0

--- a/solution.py
+++ b/solution.py
@@ -1,7 +1,408 @@
+import functools
+
 import jax
 import jax.numpy as jnp
 from jax import lax
+from jax.experimental import pallas as pl
+from jax.experimental.pallas import tpu as pltpu
 from jax.sharding import PartitionSpec as P
+
+MESH = pl.DeviceIdType.MESH
+
+
+class Place:
+    def __init__(self, n_seq, n_exp):
+        s, e = lax.axis_index("seq"), lax.axis_index("exp")
+        self.fold, self.n_exp = n_exp // 4, n_exp
+        self.length = (n_seq // 2) * self.fold
+        self.p = (s // 2) * self.fold + e // 4
+        self.x, self.y, self.c = s % 2, (e // 2) % 2, e % 2
+
+    def ids(self, p, x, y, c):
+        return (p // self.fold) * 2 + x, (p % self.fold) * 4 + y * 2 + c
+
+    def block(self, p, x, y, c):
+        s, e = self.ids(p, x, y, c)
+        return s * self.n_exp + e
+
+    def dev(self, dp=0, dx=0, dy=0, dc=0):
+        x = 1 - self.x if dx else self.x
+        y = 1 - self.y if dy else self.y
+        c = 1 - self.c if dc else self.c
+        return self.ids(self.p + dp, x, y, c)
+
+    def greet(self):
+        barrier = pltpu.get_barrier_semaphore()
+        for d in (dict(dx=1), dict(dy=1), dict(dc=1)):
+            pl.semaphore_signal(barrier, inc=1, device_id=self.dev(**d), device_id_type=MESH)
+
+        @pl.when(self.p > 0)
+        def _():
+            pl.semaphore_signal(barrier, inc=1, device_id=self.dev(dp=-1), device_id_type=MESH)
+
+        @pl.when(self.p < self.length - 1)
+        def _():
+            pl.semaphore_signal(barrier, inc=1, device_id=self.dev(dp=1), device_id_type=MESH)
+
+        ends = (self.p > 0).astype(jnp.int32) + (self.p < self.length - 1).astype(jnp.int32)
+        pl.semaphore_wait(barrier, 3 + ends)
+
+    def at(self, stage, sign, k):
+        if sign == 0:
+            stage(0, 0, 0)
+        elif sign < 0:
+            pl.when(self.p >= k)(lambda: stage(2 * k - 1, -k, -1))
+        else:
+            pl.when(self.p + k < self.length)(lambda: stage(2 * k, k, 1))
+
+    def far_first(self, stage):
+        def one(i, carry):
+            for sign in (1, -1):
+                self.at(stage, sign, self.length - 1 - i)
+            return carry
+
+        if self.length <= 8:
+            for i in range(self.length - 1):
+                one(i, 0)
+        else:
+            lax.fori_loop(0, self.length - 1, one, 0)
+        self.at(stage, 0, 0)
+
+    def near_first(self, *stages):
+        depth = len(stages)
+
+        def ring(stage, k):
+            if isinstance(k, int) and k == 0:
+                self.at(stage, 0, 0)
+            else:
+                for sign in (-1, 1):
+                    self.at(stage, sign, k)
+
+        def step(k):
+            for j, stage in enumerate(stages):
+                if 0 <= k - j < self.length:
+                    ring(stage, k - j)
+
+        total = self.length + depth - 1
+        if self.length <= 8:
+            for k in range(total):
+                step(k)
+            return
+        for k in range(depth):
+            step(k)
+
+        def one(k, carry):
+            for j, stage in enumerate(stages):
+                ring(stage, k - j)
+            return carry
+
+        lax.fori_loop(depth, self.length, one, 0)
+        for k in range(self.length, total):
+            step(k)
+
+
+def gather_kernel(n_seq, n_exp, x_ref, g_ref, out_ref, gout_ref, send, recv, loc):
+    me = Place(n_seq, n_exp)
+    rows, width = x_ref.shape
+    grow = g_ref.shape[0]
+    me.greet()
+
+    def place(ref, off, dx, dy, dc=0):
+        x = 1 - me.x if dx else me.x
+        y = 1 - me.y if dy else me.y
+        c = 1 - me.c if dc else me.c
+        b = me.block(me.p + off, x, y, c)
+        n = rows if ref is out_ref else grow
+        return ref.at[pl.ds(pl.multiple_of(b * n, n), n)]
+
+    def copies(kind, slot, off, dx, dy, to, own=False, half=None, dc=0):
+        dst_x, dst_g = place(out_ref, off, dx, dy, dc), place(gout_ref, off, dx, dy, dc)
+        src_x, src_g = (x_ref, g_ref) if own else (dst_x, dst_g)
+        if half is not None:
+            cols = pl.ds(half * (width // 2), width // 2)
+            src_x, dst_x = src_x.at[:, cols], dst_x.at[:, cols]
+        out = [
+            pltpu.make_async_remote_copy(
+                src_x, dst_x, send.at[kind, slot, 0], recv.at[kind, slot, 0], to, MESH
+            )
+        ]
+        if half != 1:
+            out.append(
+                pltpu.make_async_remote_copy(
+                    src_g, dst_g, send.at[kind, slot, 1], recv.at[kind, slot, 1], to, MESH
+                )
+            )
+        return out
+
+    def start(*a, **k):
+        for cp in copies(*a, **k):
+            cp.start()
+
+    def wait_recv(*a, **k):
+        for cp in copies(*a, **k):
+            cp.wait_recv()
+
+    def wait_send(*a, **k):
+        for cp in copies(*a, **k):
+            cp.wait_send()
+
+    left, right = dict(dp=-1), dict(dp=1)
+    X, Y, C = me.dev(dx=1), me.dev(dy=1), me.dev(dc=1)
+
+    def line_sends(off, sign, do):
+        own = sign == 0
+        if sign <= 0:
+            pl.when(me.p + 1 < me.length)(
+                lambda: do(0, 2 * (-off + 1) - 1, off, 0, 0, me.dev(**right), own=own)
+            )
+        if sign >= 0:
+            pl.when(me.p > 0)(lambda: do(0, 2 * (off + 1), off, 0, 0, me.dev(**left), own=own))
+
+    def stage_line(slot, off, sign, do):
+        own = sign == 0
+        line_sends(off, sign, do)
+        do(1, slot, off, 0, 0, X, own=own)
+        do(2, slot, off, 0, 0, Y, own=own)
+        do(5, slot, off, 0, 0, C, own=own)
+
+    def stage_xy_1(slot, off, do):
+        do(3, slot, off, 1, 0, Y, half=0)
+        do(6, slot, off, 1, 0, C)
+
+    def stage_xy_2(slot, off, do):
+        do(4, slot, off, 0, 1, X, half=1)
+        do(7, slot, off, 0, 1, C)
+
+    def stage_diag(slot, off, do):
+        do(8, slot, off, 1, 1, C)
+
+    local = [
+        pltpu.make_async_copy(x_ref, place(out_ref, 0, 0, 0), loc.at[0]),
+        pltpu.make_async_copy(g_ref, place(gout_ref, 0, 0, 0), loc.at[1]),
+    ]
+    for cp in local:
+        cp.start()
+
+    def s1(slot, off, sign):
+        if sign:
+            wait_recv(0, slot, off, 0, 0, X)
+        stage_line(slot, off, sign, start)
+
+    def s2(slot, off, sign):
+        wait_recv(1, slot, off, 1, 0, X)
+        stage_xy_1(slot, off, start)
+        wait_recv(2, slot, off, 0, 1, X)
+        stage_xy_2(slot, off, start)
+
+    def s3(slot, off, sign):
+        wait_recv(3, slot, off, 1, 1, X, half=0)
+        wait_recv(4, slot, off, 1, 1, X, half=1)
+        stage_diag(slot, off, start)
+
+    me.near_first(s1, s2, s3)
+
+    def s4(slot, off, sign):
+        stage_line(slot, off, sign, wait_send)
+        stage_xy_1(slot, off, wait_send)
+        stage_xy_2(slot, off, wait_send)
+        stage_diag(slot, off, wait_send)
+        wait_recv(5, slot, off, 0, 0, X, dc=1)
+        wait_recv(6, slot, off, 1, 0, X, dc=1)
+        wait_recv(7, slot, off, 0, 1, X, dc=1)
+        wait_recv(8, slot, off, 1, 1, X, dc=1)
+
+    me.near_first(s4)
+    for cp in local:
+        cp.wait()
+
+
+def gather_all(x, g, n_seq, n_exp):
+    n = n_seq * n_exp
+    length = n // 8
+    anyspace = pl.BlockSpec(memory_space=pl.ANY)
+    return pl.pallas_call(
+        functools.partial(gather_kernel, n_seq, n_exp),
+        out_shape=(
+            jax.ShapeDtypeStruct((n * x.shape[0], x.shape[1]), x.dtype),
+            jax.ShapeDtypeStruct((n * g.shape[0], g.shape[1]), g.dtype),
+        ),
+        in_specs=[anyspace, anyspace],
+        out_specs=(anyspace, anyspace),
+        scratch_shapes=[
+            pltpu.SemaphoreType.DMA((9, 2 * length + 1, 2)),
+            pltpu.SemaphoreType.DMA((9, 2 * length + 1, 2)),
+            pltpu.SemaphoreType.DMA((2,)),
+        ],
+        compiler_params=pltpu.CompilerParams(collective_id=1, has_side_effects=True),
+    )(x, g)
+
+
+def scatter_kernel(
+    n_seq, n_exp, y_ref, out_ref, acc, sib, xbuf, ybuf, dab, dbb, line, send, recv, loc
+):
+    me = Place(n_seq, n_exp)
+    L = me.length
+    rows, width = out_ref.shape
+    halfw = width // 2
+    me.greet()
+    X, Y, C = me.dev(dx=1), me.dev(dy=1), me.dev(dc=1)
+
+    def src(off, grp, dc):
+        x = 1 - me.x if grp & 1 else me.x
+        y = 1 - me.y if grp & 2 else me.y
+        c = 1 - me.c if dc else me.c
+        b = me.block(me.p + off, x, y, c)
+        return y_ref.at[pl.ds(pl.multiple_of(b * rows, rows), rows)]
+
+    def sib_copy(slot, off, grp):
+        return pltpu.make_async_remote_copy(
+            src(off, grp, 1), sib.at[grp, slot], send.at[grp, slot], recv.at[grp, slot], C, MESH
+        )
+
+    def load(slot, off, grp):
+        return pltpu.make_async_copy(src(off, grp, 0), acc.at[grp, slot], loc.at[grp, slot])
+
+    for grp in (3, 1, 2, 0):
+
+        def go(slot, off, sign, grp=grp):
+            sib_copy(slot, off, grp).start()
+            load(slot, off, grp).start()
+
+        me.far_first(go)
+
+    f32 = jnp.float32
+
+    def pair_sum(slot, off, grp):
+        load(slot, off, grp).wait()
+        sib_copy(slot, off, grp).wait_recv()
+        return acc[grp, slot].astype(f32) + sib[grp, slot].astype(f32)
+
+    def diag_a(slot):
+        return pltpu.make_async_remote_copy(
+            acc.at[3, slot, :, pl.ds(0, halfw)], dab.at[slot], send.at[4, slot], recv.at[4, slot], Y, MESH
+        )
+
+    def diag_b(slot):
+        return pltpu.make_async_remote_copy(
+            acc.at[3, slot, :, pl.ds(halfw, halfw)], dbb.at[slot], send.at[5, slot], recv.at[5, slot], X, MESH
+        )
+
+    def x_copy(slot):
+        return pltpu.make_async_remote_copy(
+            acc.at[1, slot], xbuf.at[slot], send.at[6, slot], recv.at[6, slot], X, MESH
+        )
+
+    def y_copy(slot):
+        return pltpu.make_async_remote_copy(
+            acc.at[2, slot], ybuf.at[slot], send.at[7, slot], recv.at[7, slot], Y, MESH
+        )
+
+    def line_copy(slot, sign):
+        return pltpu.make_async_remote_copy(
+            acc.at[0, slot],
+            line.at[slot],
+            send.at[8, slot],
+            recv.at[8, slot],
+            me.dev(dp=sign),
+            MESH,
+        )
+
+    def d1(slot, off, sign):
+        acc[3, slot] = pair_sum(slot, off, 3).astype(acc.dtype)
+        diag_a(slot).start()
+        diag_b(slot).start()
+
+    def d2(slot, off, sign):
+        sx = pair_sum(slot, off, 1)
+        diag_a(slot).wait_recv()
+        acc[1, slot, :, pl.ds(0, halfw)] = (sx[:, :halfw] + dab[slot].astype(f32)).astype(acc.dtype)
+        acc[1, slot, :, pl.ds(halfw, halfw)] = sx[:, halfw:].astype(acc.dtype)
+        x_copy(slot).start()
+        sy = pair_sum(slot, off, 2)
+        diag_b(slot).wait_recv()
+        acc[2, slot, :, pl.ds(0, halfw)] = sy[:, :halfw].astype(acc.dtype)
+        acc[2, slot, :, pl.ds(halfw, halfw)] = (sy[:, halfw:] + dbb[slot].astype(f32)).astype(acc.dtype)
+        y_copy(slot).start()
+
+    def d3(slot, off, sign):
+        total = pair_sum(slot, off, 0)
+        x_copy(slot).wait_recv()
+        y_copy(slot).wait_recv()
+        total = total + xbuf[slot].astype(f32) + ybuf[slot].astype(f32)
+        if sign == 0:
+            out_ref[...] = total
+            if L > 1:
+
+                @pl.when(me.p > 0)
+                def _():
+                    in_copy(2).wait_recv()
+                    out_ref[...] += line[2].astype(f32)
+
+                @pl.when(me.p < L - 1)
+                def _():
+                    in_copy(1).wait_recv()
+                    out_ref[...] += line[1].astype(f32)
+
+            return
+        acc[0, slot] = total.astype(acc.dtype)
+        far = slot + 2
+        behind = me.p > 0 if sign > 0 else me.p < L - 1
+
+        @pl.when(jnp.logical_and(behind, sign * off + 1 < L))
+        def _():
+            in_copy(far).wait_recv()
+            acc[0, slot] = (acc[0, slot].astype(f32) + line[far].astype(f32)).astype(acc.dtype)
+
+        line_copy(slot, sign).start()
+
+    def in_copy(slot):
+        return pltpu.make_async_remote_copy(
+            acc.at[0, slot], line.at[slot], send.at[8, slot], recv.at[8, slot], X, MESH
+        )
+
+    me.far_first(d1)
+    me.far_first(d2)
+    me.far_first(d3)
+
+    def fin(slot, off, sign):
+        for grp in range(4):
+            sib_copy(slot, off, grp).wait_send()
+        diag_a(slot).wait_send()
+        diag_b(slot).wait_send()
+        x_copy(slot).wait_send()
+        y_copy(slot).wait_send()
+        if sign:
+            line_copy(slot, sign).wait_send()
+
+    me.far_first(fin)
+
+
+def scatter_sum(part, n_seq, n_exp):
+    n = n_seq * n_exp
+    slots = n // 4 - 1 + 2
+    rows, width = part.shape[0] // n, part.shape[1]
+    bf = jnp.bfloat16
+    return pl.pallas_call(
+        functools.partial(scatter_kernel, n_seq, n_exp),
+        out_shape=jax.ShapeDtypeStruct((rows, width), jnp.float32),
+        in_specs=[pl.BlockSpec(memory_space=pl.ANY)],
+        out_specs=pl.BlockSpec(memory_space=pltpu.VMEM),
+        scratch_shapes=[
+            pltpu.VMEM((4, slots, rows, width), bf),
+            pltpu.VMEM((4, slots, rows, width), bf),
+            pltpu.VMEM((slots, rows, width), bf),
+            pltpu.VMEM((slots, rows, width), bf),
+            pltpu.VMEM((slots, rows, width // 2), bf),
+            pltpu.VMEM((slots, rows, width // 2), bf),
+            pltpu.VMEM((slots, rows, width), bf),
+            pltpu.SemaphoreType.DMA((9, slots)),
+            pltpu.SemaphoreType.DMA((9, slots)),
+            pltpu.SemaphoreType.DMA((4, slots)),
+        ],
+        compiler_params=pltpu.CompilerParams(
+            collective_id=2, has_side_effects=True, vmem_limit_bytes=60 * 2**20
+        ),
+    )(part)
 
 
 def carried_in(value, axis, join, neutral):
@@ -26,14 +427,6 @@
 
 def combine_states(earlier, later):
     return (earlier[0] + later[0], jnp.exp(later[0])[:, None, None] * earlier[1] + later[1])
-
-
-def route_targets(ids_block, experts, capacity):
-    flat_ids = ids_block.reshape(-1)
-    onehot = (flat_ids[:, None] == jnp.arange(experts, dtype=jnp.int32)[None, :]).astype(jnp.int32)
-    before = jnp.cumsum(onehot, axis=0) - onehot
-    slot_index = jnp.sum(before * onehot, axis=1)
-    return flat_ids * capacity + slot_index
 
 
 def body(
@@ -95,41 +488,45 @@
     moe_in = (
         hid32 * lax.rsqrt(jnp.mean(hid32 * hid32, axis=-1, keepdims=True) + 1e-06) * moe_gain
     ).astype(jnp.bfloat16)
-    exp_count = lax.axis_size("exp")
+    n_seq, n_exp = lax.axis_size("seq"), lax.axis_size("exp")
     tok_rows = residual.shape[0]
-    width = residual.shape[1]
-    local_experts = w_gate.shape[0]
-    experts = local_experts * exp_count
-    capacity = max(2, (3 * tok_rows + experts - 1) // experts)
-    slots = experts * capacity
-    slot_range = jnp.arange(slots, dtype=jnp.int32)
-    target = route_targets(expert_ids, experts, capacity)
-    selector = (target[None, :] == slot_range[:, None]).astype(jnp.bfloat16)
-    doubled = jnp.repeat(moe_in, 2, axis=0)
-    outgoing = jnp.dot(selector, doubled, preferred_element_type=jnp.float32).astype(jnp.bfloat16)
-    outgoing = outgoing.reshape(exp_count, local_experts, capacity, width)
-    arrived = lax.all_to_all(outgoing, "exp", split_axis=0, concat_axis=0, tiled=True)
-    piece = lax.all_gather(arrived, "seq", axis=0, tiled=True)
-    gate_part = jnp.einsum("ajcd,jfd->ajcf", piece, w_gate, preferred_element_type=jnp.float32)
-    up_part = jnp.einsum("ajcd,jfd->ajcf", piece, w_up, preferred_element_type=jnp.float32)
-    active = (jax.nn.silu(gate_part) * up_part).astype(jnp.bfloat16)
-    piece = active
-    summed = lax.psum_scatter(
-        jnp.einsum("ajcf,jfd->ajcd", piece, w_down, preferred_element_type=jnp.float32).astype(
-            jnp.bfloat16
+    experts = w_gate.shape[0] * n_exp
+    gates = jnp.sum(
+        jnp.where(
+            expert_ids[:, :, None] == jnp.arange(experts, dtype=jnp.int32)[None, None, :],
+            gate_weights[:, :, None],
+            0.0,
         ),
-        "seq",
-        scatter_dimension=0,
-        tiled=True,
-    )
-    returned = lax.all_to_all(summed, "exp", split_axis=0, concat_axis=0, tiled=True)
-    flat_back = returned.reshape(slots, width)
-    picked = lax.dot_general(
-        selector, flat_back, (((0,), (0,)), ((), ())), preferred_element_type=jnp.float32
-    )
-    picked = picked.reshape(tok_rows, 2, width)
-    mixed = hid32 + jnp.sum(gate_weights[:, :, None] * picked, axis=1)
-    return mixed.astype(jnp.bfloat16)
+        axis=1,
+    )
+    flat = gates.T.reshape(-1)
+    pad = -flat.shape[0] % 1024
+    g_tile = jnp.pad(flat, (0, pad)).reshape(-1, 128)
+    everyone, g_all = gather_all(moe_in, g_tile, n_seq, n_exp)
+    g_all = g_all.reshape(n_seq * n_exp, -1)[:, : experts * tok_rows]
+    g_all = g_all.reshape(n_seq * n_exp, experts, tok_rows)
+    mixed = None
+    gate_col = lax.dynamic_slice_in_dim(
+        g_all, lax.axis_index("exp") * w_gate.shape[0], w_gate.shape[0], 1
+    )
+    part = None
+    for j in range(w_gate.shape[0]):
+        gate_part = jnp.einsum("td,fd->tf", everyone, w_gate[j], preferred_element_type=jnp.float32)
+        up_part = jnp.einsum("td,fd->tf", everyone, w_up[j], preferred_element_type=jnp.float32)
+        active = (
+            jax.nn.silu(gate_part) * up_part * gate_col[:, j, :].reshape(-1, 1)
+        ).astype(jnp.bfloat16)
+        one = jnp.dot(active, w_down[j], preferred_element_type=jnp.float32)
+        part = one if part is None else part + one
+    part = part.astype(jnp.bfloat16)
+    total_rows, width = part.shape
+    pieces = max(1, total_rows // 1024)
+    step = width // pieces
+    summed = [
+        jax.jit(scatter_sum, static_argnums=(1, 2))(part[:, i * step : (i + 1) * step], n_seq, n_exp) for i in range(pieces)
+    ]
+    summed = summed[0] if pieces == 1 else jnp.concatenate(summed, axis=1)
+    return (hid32 + summed).astype(jnp.bfloat16)
 
 
 def solution(mesh):

time: 372 us -> 228 us (0.61)
  waiting for transfers between devices: 266 us -> 34.8 us
  Pallas kernels: 0 us -> 94.8 us
  blocking collectives: 37 us -> 22.3 us
  matrix products: 41 us -> 49.8 us
  starting transfers between devices: 7.17 us -> 3.44 us
    reduce_scatter x1 -> x0, waiting for transfers between devices: 116 us -> none  [body(): lax.psum_scatter(jnp.einsum('ajcf,jfd->ajcd', piece, w_down, preferred_el...]
    all_gather x1 -> x0, waiting for transfers between devices: 104 us -> none  [body(): piece = lax.all_gather(arrived, 'seq', axis=0, tiled=True)]
    pallas_call x0 -> x2, Pallas kernels: none -> 94.8 us  [the longest x1 48.3 us: gather_all(): pl.pallas_call(functools.partial(gather_kernel, n_seq, n_exp), out_shape=...]
    all_to_all x1 -> x0, blocking collectives: 14.7 us -> none  [body(): lax.all_to_all(outgoing, 'exp', split_axis=0, concat_axis=0, tiled=True)]
    all_to_all x1 -> x0, waiting for transfers between devices: 11.4 us -> none  [body(): lax.all_to_all(summed, 'exp', split_axis=0, concat_axis=0, tiled=True)]
    dot_general x5 -> x3, matrix products: 38.9 us -> 47.7 us  [the longest x1 17.8 us: body(): jnp.einsum('td,fd->tf', everyone, w_gate[j], preferred_element_type=jnp.f...]
  transfers between devices with their start and end apart: 5 -> 2, of which waited for: 5 -> 2; matrix products, arithmetic and copies ran while one was open for 0% -> 0% of each run, Pallas kernels for 0% -> 0%
where the time goes in v1:
time: 228 us; the launch traced here: 227 us
  Pallas kernels  94.8 us (42%)
  matrix products  49.8 us (22%)
  waiting for transfers between devices  34.8 us (15%)
  blocking collectives  22.3 us (10%)
  between operations  13.6 us (6%)
  local copies, waits for them, and re-layouts  5.14 us (2%)
  starting transfers between devices  3.44 us (2%)
  other arithmetic  3.22 us (1%)
    pallas_call x1, Pallas kernels, gather_all(): pl.pallas_call(functools.partial(gather_kernel, n_seq, n_exp), out_shape=...  48.3 us
    pallas_call x1, Pallas kernels, scatter_sum(): pl.pallas_call(functools.partial(scatter_kernel, n_seq, n_exp), out_shape...  46.5 us
    all_gather x1, waiting for transfers between devices, carried_in(): lax.all_gather(a.astype(kind), axis)  29.5 us
    all_gather x1, blocking collectives, carried_in(): lax.all_gather(a.astype(kind), axis)  22.3 us
    dot_general x1, matrix products, body(): jnp.einsum('td,fd->tf', everyone, w_gate[j], preferred_element_type=jnp.f...  17.8 us
    dot_general x1, matrix products, body(): jnp.einsum('td,fd->tf', everyone, w_up[j], preferred_element_type=jnp.flo...  17 us
    dot_general x1, matrix products, body(): one = jnp.dot(active, w_down[j], preferred_element_type=jnp.float32)  13 us
    all_to_all x1, waiting for transfers between devices, body(): lax.all_to_all(normed, 'exp', split_axis=0, concat_axis=1, tiled=True)  5.26 us
  transfers between devices with their start and end apart: 2, of which 2 were waited for; matrix products, arithmetic and copies ran while one was open for 0% of the time, Pallas kernels for 0%

profile of v1, /device:TPU:0, one launch (start us, length us, event | category | flops | bytes accessed | tf_op | source)
XLA Modules:
  0.0 227.1 jit_solution(14288439947649086001)
XLA Ops:
  6.5 0.0 copy-start
  6.5 0.0 copy-start.1
  6.5 0.0 copy-start.5
  6.5 0.0 copy-start.6
  6.5 0.0 all-gather.4.cloned.1.call-start
  6.6 0.8 copy.58
  7.4 0.2 reduce_window_sum.11
  7.7 0.0 copy-start.2
  7.7 0.0 copy-start.3
  7.7 1.2 copy.72
  8.9 0.0 copy-done
  8.9 0.9 convolution_convert_fusion
  9.8 0.0 copy-start.4
  9.8 0.0 all-gather.4.cloned.1.call-update
  9.9 22.3 %all-gather.1 = bf16[8,1,8]{2,1,0:T(2,128)(2,1)S(1)} all-gather(bf16[1,1,8]{2,1,0:T(2,128)(2,1)S(1)} %convert_bitcast_fusion.1), channel_id=1, replica_groups=mesh['seq'=8,'exp'=4] {'seq'}, dimensions={0}, use_global_device_ids=true | all-gather | bytes 144 | tf_op jit(solution)/shard_map/all_gather | solution.py:411
  32.2 0.1 copy.62
  32.3 29.5 %all-gather.4.cloned.1.call-done = bf16[64,128,128]{2,1,0:T(8,128)(2,1)} async-done(((bf16[8,128,128]{2,1,0:T(8,128)(2,1)}), bf16[64,128,128]{2,1,0:T(8,128)(2,1)}) %all-gather.4.cloned.1.call-update) | async-done | bytes 2097168 | tf_op jit(solution)/shard_map/all_gather | solution.py:411
  61.9 0.0 copy-done.1
  61.9 0.6 fusion.20
  62.5 0.5 multiply_reduce_fusion
  63.0 0.2 copy.68
  63.2 0.8 all_to_all.10
  64.1 3.4 %all-to-all-start = ((bf16[4,32,1024]{2,1,0:T(8,128)(2,1)}), bf16[4,32,1024]{2,1,0:T(8,128)(2,1)S(1)}, u32[]{:S(2)}, u32[]{:S(2)}) async-start(bf16[4,32,1024]{2,1,0:T(8,128)(2,1)} %all_to_all.10), calls=%async_computation | async-start | bytes 524288 | tf_op jit(solution)/shard_map/all_to_all | solution.py:483
  67.5 0.0 copy-done.5
  67.5 0.0 copy-done.6
  67.5 0.1 reshape.91
  67.6 0.6 pad_bitcast_fusion.g_ref
  68.2 5.3 %all-to-all-done = bf16[4,32,1024]{2,1,0:T(8,128)(2,1)S(1)} async-done(((bf16[4,32,1024]{2,1,0:T(8,128)(2,1)}), bf16[4,32,1024]{2,1,0:T(8,128)(2,1)S(1)}, u32[]{:S(2)}, u32[]{:S(2)}) %all-to-all-start) | async-done | bytes 262176 | tf_op jit(solution)/shard_map/all_to_all | solution.py:483
  73.5 0.0 copy-done.2
  73.5 0.0 copy-done.3
  73.6 0.2 fusion.22
  73.8 0.0 copy-done.4
  73.8 0.8 fusion.24.x_ref
  74.6 48.3 %shard_map.118 = (bf16[1024,4096]{1,0:T(8,128)(2,1)}, f32[256,128]{1,0:T(8,128)}) custom-call(bf16[32,4096]{1,0:T(8,128)(2,1)} %fusion.24.x_ref, f32[8,128]{1,0:T(8,128)} %pad_bitcast_fusion.g_ref), custom_call_target="tpu_custom_call" | custom-call | tf_op jit(solution)/shard_map/pallas_call | solution.py:223
  123.0 0.9 reshape.93
  123.9 0.1 reshape.94
  124.0 0.1 dynamic-slice_reduce_fusion
  124.1 0.1 mul.103
  124.1 0.0 slice-start
  124.1 0.0 slice-start.1
  124.1 17.8 %fusion.4 = f32[1024,1152]{1,0:T(8,128)} fusion(bf16[1024,4096]{1,0:T(8,128)(2,1)} %get-tuple-element.52, bf16[1,1152,4096]{2,1,0:T(8,128)(2,1)} %param.23), kind=kOutput, calls=%fused_computation.6 | convolution fusion | flops 9663676416 | bytes 22544384 | tf_op jit(solution)/shard_map/td,fd->tf/dot_general | solution.py:514
  141.9 0.0 slice-start.2
  141.9 17.0 %fusion.15 = bf16[1024,1152]{1,0:T(8,128)(2,1)S(1)} fusion(bf16[1024,4096]{1,0:T(8,128)(2,1)} %get-tuple-element.52, bf16[1,1152,4096]{2,1,0:T(8,128)(2,1)} %param.24, f32[1024,1152]{1,0:T(8,128)} %fusion.4, f32[1024]{0:T(1024)S(1)} %mul.103), kind=kOutput, calls=%fused_computation.11 | convolution fusion | flops 9671933952 | bytes 24907776 | tf_op jit(solution)/shard_map/td,fd->tf/dot_general | solution.py:515
  159.0 0.0 slice-done
  159.0 0.0 slice-done.1
  159.0 0.0 slice-done.2
  159.0 13.0 %fusion.6.y_ref = bf16[1024,4096]{1,0:T(8,128)(2,1)} fusion(bf16[1024,1152]{1,0:T(8,128)(2,1)S(1)} %fusion.15, bf16[1,1152,4096]{2,1,0:T(8,128)(2,1)S(1)} %bitcast.94), kind=kOutput, calls=%fused_computation.8 | convolution fusion | flops 9667870720 | bytes 20185088 | tf_op jit(solution)/shard_map/dot_general | solution.py:519
  171.9 46.5 %scatter_sum.1 = f32[32,4096]{1,0:T(8,128)} custom-call(bf16[1024,4096]{1,0:T(8,128)(2,1)} %fusion.6.y_ref), custom_call_target="tpu_custom_call" | custom-call | tf_op jit(solution)/shard_map/jit(scatter_sum)/pallas_call | solution.py:385
  218.4 1.8 fusion.25
  (17 shorter events, 0.4 us)
Async XLA Ops:
  6.5 2.3 %copy-start = (bf16[128,1024]{1,0:T(8,128)(2,1)S(1)}, bf16[128,1024]{1,0:T(8,128)(2,1)}, u32[]{:S(2)}) copy-start(bf16[128,1024]{1,0:T(8,128)(2,1)} %param.16) | copy-start | bytes 786436
  6.5 55.3 %copy-start.1 = (bf16[128,1024]{1,0:T(8,128)(2,1)S(1)}, bf16[128,1024]{1,0:T(8,128)(2,1)}, u32[]{:S(2)}) copy-start(bf16[128,1024]{1,0:T(8,128)(2,1)} %param.14) | copy-start | bytes 786436
  6.5 60.9 %copy-start.5 = (f32[32,2]{0,1:T(2,128)S(1)}, f32[32,2]{0,1:T(2,128)}, u32[]{:S(2)}) copy-start(f32[32,2]{0,1:T(2,128)} %param.22) | copy-start | bytes 772
  6.5 60.9 %copy-start.6 = (s32[32,2]{0,1:T(2,128)S(1)}, s32[32,2]{0,1:T(2,128)}, u32[]{:S(2)}) copy-start(s32[32,2]{0,1:T(2,128)} %param.21) | copy-start | bytes 772
  6.5 55.2 %all-gather.4.cloned.1.call-start = ((), (), s32[]{:S(2)}) async-start(), calls=%async_computation.1 | async-start | bytes 2359296 | tf_op jit(solution)/shard_map/all_gather | solution.py:411
  7.7 65.9 %copy-start.2 = (bf16[32,4096]{1,0:T(8,128)(2,1)S(1)}, bf16[32,4096]{1,0:T(8,128)(2,1)}, u32[]{:S(2)}) copy-start(bf16[32,4096]{1,0:T(8,128)(2,1)} %param.18) | copy-start | bytes 786436
  7.7 65.9 %copy-start.3 = (f32[4096]{0:T(1024)S(1)}, f32[4096]{0:T(1024)}, u32[]{:S(2)}) copy-start(f32[4096]{0:T(1024)} %param.19) | copy-start | bytes 49156
  9.8 64.0 %copy-start.4 = (f32[4096]{0:T(1024)S(1)}, f32[4096]{0:T(1024)}, u32[]{:S(2)}) copy-start(f32[4096]{0:T(1024)} %param.20) | copy-start | bytes 49156
  64.1 9.4 %all-to-all-start = ((bf16[4,32,1024]{2,1,0:T(8,128)(2,1)}), bf16[4,32,1024]{2,1,0:T(8,128)(2,1)S(1)}, u32[]{:S(2)}, u32[]{:S(2)}) async-start(bf16[4,32,1024]{2,1,0:T(8,128)(2,1)} %all_to_all.10), calls=%async_computation | async-start | bytes 524288 | tf_op jit(solution)/shard_map/all_to_all | solution.py:483
  124.1 34.8 %slice-start = ((s8[9437184]{0:T(1024)(128)(4,1)}), s8[4194304]{0:T(1024)(128)(4,1)S(1)}, s32[]{:S(2)}) async-start(s8[9437184]{0:T(1024)(128)(4,1)} %bitcast.93), calls=%async_computation.2 | async-start | bytes 8388608
  124.1 34.8 %slice-start.1 = ((s8[9437184]{0:T(1024)(128)(4,1)}), s8[1048576]{0:T(1024)(128)(4,1)S(1)}, s32[]{:S(2)}) async-start(s8[9437184]{0:T(1024)(128)(4,1)} %bitcast.93), calls=%async_computation.3 | async-start | bytes 2097152
  141.9 17.0 %slice-start.2 = ((s8[9437184]{0:T(1024)(128)(4,1)}), s8[4194304]{0:T(1024)(128)(4,1)S(1)}, s32[]{:S(2)}) async-start(s8[9437184]{0:T(1024)(128)(4,1)} %bitcast.93), calls=%async_computation.4 | async-start | bytes 8388608
Sparse Core Ops, SparseCore 0:
  10.0 51.7 all-gather.3

commit v2 on v1

--- a/solution.py
+++ b/solution.py
@@ -405,28 +405,105 @@
     )(part)
 
 
-def carried_in(value, axis, join, neutral):
-    place = lax.axis_index(axis)
-    gathered = jax.tree.map(
-        lambda a, kind: lax.all_gather(a.astype(kind), axis), value, (jnp.bfloat16, jnp.bfloat16)
-    )
-    state = jax.tree.map(lambda a, e: jnp.zeros_like(a) + jnp.asarray(e, a.dtype), value, neutral)
-
-    def one(hop, state):
-        return join(
-            state,
-            jax.tree.map(
-                lambda a, own: lax.dynamic_index_in_dim(a, hop, 0, False).astype(own.dtype),
-                gathered,
-                value,
-            ),
-        )
-
-    return lax.fori_loop(0, place, one, state)
-
-
-def combine_states(earlier, later):
-    return (earlier[0] + later[0], jnp.exp(later[0])[:, None, None] * earlier[1] + later[1])
+def carry_kernel(n_seq, own_ref, own16_ref, tot_ref, out_ref, peer, ptot, cin, cout, send, recv, tsem):
+    s, e = lax.axis_index("seq"), lax.axis_index("exp")
+    z, odd, deep = s // 2, s % 2, n_seq // 2
+    heads = own_ref.shape[0]
+    pair = (z * 2 + 1 - odd, e)
+
+    barrier = pltpu.get_barrier_semaphore()
+    pl.semaphore_signal(barrier, inc=1, device_id=pair, device_id_type=MESH)
+
+    @pl.when(z > 0)
+    def _():
+        pl.semaphore_signal(barrier, inc=1, device_id=(s - 2, e), device_id_type=MESH)
+
+    @pl.when(z < deep - 1)
+    def _():
+        pl.semaphore_signal(barrier, inc=1, device_id=(s + 2, e), device_id_type=MESH)
+
+    ends = (z > 0).astype(jnp.int32) + (z < deep - 1).astype(jnp.int32)
+    pl.semaphore_wait(barrier, 1 + ends)
+
+    tot_copy = pltpu.make_async_remote_copy(tot_ref, ptot, tsem.at[0], tsem.at[1], pair, MESH)
+
+    def pair_copy(h):
+        return pltpu.make_async_remote_copy(
+            own16_ref.at[h], peer.at[h], send.at[0, h], recv.at[0, h], pair, MESH
+        )
+
+    def line_copy(h):
+        return pltpu.make_async_remote_copy(
+            cout.at[h], cin.at[h], send.at[1, h], recv.at[1, h], (s + 2, e), MESH
+        )
+
+    tot_copy.start()
+    for h in range(heads):
+        pair_copy(h).start()
+
+    @pl.when(z == 0)
+    def _():
+        cin[...] = jnp.zeros_like(cin)
+
+    tot_copy.wait_recv()
+    mine, other = tot_ref[...], ptot[...]
+    both = jnp.exp(mine + other)
+    is_odd = jnp.full(mine.shape, odd, jnp.int32) == 1
+    one = jnp.ones_like(mine)
+    own_by = jnp.where(is_odd, one, jnp.exp(other))
+    peer_by = jnp.where(is_odd, jnp.exp(mine), one)
+    carry_by = jnp.where(is_odd, jnp.exp(other), one)
+    peer_in = jnp.where(is_odd, one, jnp.zeros_like(mine))
+    for h in range(heads):
+        pair_copy(h).wait_recv()
+
+        @pl.when(z > 0)
+        def _():
+            line_copy(h).wait_recv()
+
+        near = peer[h].astype(jnp.float32)
+        come = cin[h].astype(jnp.float32)
+
+        @pl.when(z < deep - 1)
+        def _():
+            cout[h] = (
+                both[h : h + 1] * come + own_by[h : h + 1] * own_ref[h] + peer_by[h : h + 1] * near
+            ).astype(cout.dtype)
+            line_copy(h).start()
+
+        out_ref[h] = carry_by[h : h + 1] * come + peer_in[h : h + 1] * near
+
+    tot_copy.wait_send()
+    for h in range(heads):
+        pair_copy(h).wait_send()
+
+        @pl.when(z < deep - 1)
+        def _():
+            line_copy(h).wait_send()
+
+
+def carried_in(block_total, block_state, n_seq):
+    heads, dim, _ = block_state.shape
+    bf = jnp.bfloat16
+    tile = jnp.pad(block_total, (0, -heads % 8))
+    tile = jnp.broadcast_to(tile[:, None], (tile.shape[0], dim))
+    vmem = pl.BlockSpec(memory_space=pltpu.VMEM)
+    return pl.pallas_call(
+        functools.partial(carry_kernel, n_seq),
+        out_shape=jax.ShapeDtypeStruct(block_state.shape, jnp.float32),
+        in_specs=[vmem] * 3,
+        out_specs=vmem,
+        scratch_shapes=[
+            pltpu.VMEM(block_state.shape, bf),
+            pltpu.VMEM(tile.shape, jnp.float32),
+            pltpu.VMEM(block_state.shape, bf),
+            pltpu.VMEM(block_state.shape, bf),
+            pltpu.SemaphoreType.DMA((2, heads)),
+            pltpu.SemaphoreType.DMA((2, heads)),
+            pltpu.SemaphoreType.DMA((2,)),
+        ],
+        compiler_params=pltpu.CompilerParams(collective_id=3, has_side_effects=True),
+    )(block_state, block_state.astype(bf), tile)
 
 
 def body(
@@ -457,11 +534,7 @@
     block_state = jnp.einsum(
         "thd,the->hde", keys_weighted, v_heads, preferred_element_type=jnp.float32
     )
-    identity_pair = (
-        jnp.zeros((heads,), jnp.float32),
-        jnp.zeros((heads, head_dim, head_dim), jnp.float32),
-    )
-    carried = carried_in((block_total, block_state), "seq", combine_states, identity_pair)[1]
+    carried = carried_in(block_total, block_state, lax.axis_size("seq"))
     scores = jnp.einsum("thd,shd->hts", q_heads, k_heads, preferred_element_type=jnp.float32)
     gap_logs = log_cum.T[:, :, None] - log_cum.T[:, None, :]
     causal_mask = (

time: 228 us -> 179 us (0.79)
  waiting for transfers between devices: 34.8 us -> 5.25 us
  blocking collectives: 22.3 us -> 0 us
  Pallas kernels: 94.8 us -> 109 us
  between operations: 13.6 us -> 0.25 us
    all_gather x1 -> x0, waiting for transfers between devices: 29.5 us -> none  [carried_in(): lax.all_gather(a.astype(kind), axis)]
    all_gather x1 -> x0, blocking collectives: 22.3 us -> none  [carried_in(): lax.all_gather(a.astype(kind), axis)]
    pallas_call x0 -> x1, Pallas kernels: none -> 14.5 us  [carried_in(): pl.pallas_call(functools.partial(carry_kernel, n_seq), out_shape=jax.Shap...]
  transfers between devices with their start and end apart: 2 -> 1, of which waited for: 2 -> 1; matrix products, arithmetic and copies ran while one was open for 0% -> 0% of each run, Pallas kernels for 0% -> 0%
where the time goes in v2:
time: 179 us
  Pallas kernels  109 us (61%)
  matrix products  52 us (29%)
  local copies, waits for them, and re-layouts  5.75 us (3%)
  waiting for transfers between devices  5.25 us (3%)
  starting transfers between devices  3.41 us (2%)
  other arithmetic  3.18 us (2%)
    pallas_call x1, Pallas kernels, gather_all(): pl.pallas_call(functools.partial(gather_kernel, n_seq, n_exp), out_shape=...  48.2 us
    pallas_call x1, Pallas kernels, scatter_sum(): pl.pallas_call(functools.partial(scatter_kernel, n_seq, n_exp), out_shape...  46.4 us
    dot_general x1, matrix products, body(): jnp.einsum('td,fd->tf', everyone, w_gate[j], preferred_element_type=jnp.f...  17.8 us
    dot_general x1, matrix products, body(): jnp.einsum('td,fd->tf', everyone, w_up[j], preferred_element_type=jnp.flo...  17 us
    pallas_call x1, Pallas kernels, carried_in(): pl.pallas_call(functools.partial(carry_kernel, n_seq), out_shape=jax.Shap...  14.5 us
    dot_general x1, matrix products, body(): one = jnp.dot(active, w_down[j], preferred_element_type=jnp.float32)  13 us
    all_to_all x1, waiting for transfers between devices, body(): lax.all_to_all(normed, 'exp', split_axis=0, concat_axis=1, tiled=True)  5.25 us
  transfers between devices with their start and end apart: 1, of which 1 were waited for; matrix products, arithmetic and copies ran while one was open for 0% of the time, Pallas kernels for 0%

profile of v2, /device:TPU:0, one launch (start us, length us, event | category | flops | bytes accessed | tf_op | source)
XLA Modules:
  0.0 179.0 jit_solution(6188467175225538755)
XLA Ops:
  0.0 0.0 copy-start
  0.0 0.0 copy-start.4
  0.0 0.0 copy-start.5
  0.0 0.0 copy-start.2
  0.0 0.0 copy-start.1
  0.0 0.0 copy-start.3
  0.1 0.9 copy.42
  0.9 0.2 reduce_window_sum.11
  1.2 0.1 copy.48
  1.3 1.1 copy.55
  2.5 0.0 copy-done
  2.5 1.1 fusion.47
  3.6 0.7 broadcast_in_dim.50.tot_ref
  4.2 14.5 %shard_map.118 = f32[8,128,128]{2,1,0:T(8,128)} custom-call(f32[8,128,128]{2,1,0:T(8,128)} %get-tuple-element.14.own_ref, bf16[8,128,128]{2,1,0:T(8,128)(2,1)} %get-tuple-element.13.own16_ref, f32[8,128]{1,0:T(8,128)} %broadcast_in_dim.50.tot_ref), custom_call_target="tpu_custom_call" | custom-call | tf_op jit(solution)/shard_map/pallas_call | solution.py:491
  18.8 1.7 fusion.20
  20.5 1.5 multiply_reduce_fusion
  22.0 0.2 copy.52
  22.2 0.8 all_to_all.10
  23.0 3.4 %all-to-all-start = ((bf16[4,32,1024]{2,1,0:T(8,128)(2,1)}), bf16[4,32,1024]{2,1,0:T(8,128)(2,1)S(1)}, u32[]{:S(2)}, u32[]{:S(2)}) async-start(bf16[4,32,1024]{2,1,0:T(8,128)(2,1)} %all_to_all.10), calls=%async_computation | async-start | bytes 524288 | tf_op jit(solution)/shard_map/all_to_all | solution.py:556
  26.4 0.0 copy-done.4
  26.4 0.0 copy-done.5
  26.5 0.1 reshape.83
  26.5 0.6 pad_bitcast_fusion.g_ref
  27.1 5.3 %all-to-all-done = bf16[4,32,1024]{2,1,0:T(8,128)(2,1)S(1)} async-done(((bf16[4,32,1024]{2,1,0:T(8,128)(2,1)}), bf16[4,32,1024]{2,1,0:T(8,128)(2,1)S(1)}, u32[]{:S(2)}, u32[]{:S(2)}) %all-to-all-start) | async-done | bytes 262176 | tf_op jit(solution)/shard_map/all_to_all | solution.py:556
  32.5 0.0 copy-done.2
  32.5 0.0 copy-done.1
  32.5 0.2 fusion.22
  32.7 0.0 copy-done.3
  32.7 0.8 fusion.24.x_ref
  33.6 48.2 %shard_map.119 = (bf16[1024,4096]{1,0:T(8,128)(2,1)}, f32[256,128]{1,0:T(8,128)}) custom-call(bf16[32,4096]{1,0:T(8,128)(2,1)} %fusion.24.x_ref, f32[8,128]{1,0:T(8,128)} %pad_bitcast_fusion.g_ref), custom_call_target="tpu_custom_call" | custom-call | tf_op jit(solution)/shard_map/pallas_call | solution.py:223
  81.8 0.9 reshape.85
  82.7 0.1 reshape.86
  82.8 0.1 dynamic-slice_reduce_fusion
  82.9 0.1 mul.91
  83.0 0.0 slice-start
  83.0 0.0 slice-start.1
  83.0 17.8 %fusion.4 = f32[1024,1152]{1,0:T(8,128)} fusion(bf16[1024,4096]{1,0:T(8,128)(2,1)} %get-tuple-element.7, bf16[1,1152,4096]{2,1,0:T(8,128)(2,1)} %param.21), kind=kOutput, calls=%fused_computation.4 | convolution fusion | flops 9663676416 | bytes 22544384 | tf_op jit(solution)/shard_map/td,fd->tf/dot_general | solution.py:587
  100.8 0.0 slice-start.2
  100.8 17.0 %fusion.15 = bf16[1024,1152]{1,0:T(8,128)(2,1)S(1)} fusion(bf16[1024,4096]{1,0:T(8,128)(2,1)} %get-tuple-element.7, bf16[1,1152,4096]{2,1,0:T(8,128)(2,1)} %param.22, f32[1024,1152]{1,0:T(8,128)} %fusion.4, f32[1024]{0:T(1024)S(1)} %mul.91), kind=kOutput, calls=%fused_computation.9 | convolution fusion | flops 9671933952 | bytes 24907776 | tf_op jit(solution)/shard_map/td,fd->tf/dot_general | solution.py:588
  117.8 0.0 slice-done
  117.8 0.0 slice-done.1
  117.8 0.0 slice-done.2
  117.8 13.0 %fusion.6.y_ref = bf16[1024,4096]{1,0:T(8,128)(2,1)} fusion(bf16[1024,1152]{1,0:T(8,128)(2,1)S(1)} %fusion.15, bf16[1,1152,4096]{2,1,0:T(8,128)(2,1)S(1)} %bitcast.79), kind=kOutput, calls=%fused_computation.6 | convolution fusion | flops 9667870720 | bytes 20185088 | tf_op jit(solution)/shard_map/dot_general | solution.py:592
  130.8 46.4 %scatter_sum.1 = f32[32,4096]{1,0:T(8,128)} custom-call(bf16[1024,4096]{1,0:T(8,128)(2,1)} %fusion.6.y_ref), custom_call_target="tpu_custom_call" | custom-call | tf_op jit(solution)/shard_map/jit(scatter_sum)/pallas_call | solution.py:385
  177.2 1.8 %fusion.25 = bf16[32,4096]{1,0:T(8,128)(2,1)} fusion(f32[32,4096]{1,0:T(8,128)} %scatter_sum.1, bf16[32,4096]{1,0:T(8,128)(2,1)S(1)} %get-tuple-element.10), kind=kLoop, calls=%fused_computation.23 | loop fusion | flops 393216 | bytes 1048576 | tf_op jit(solution)/shard_map/convert_element_type | solution.py:602
  (13 shorter events, 0.3 us)
Async XLA Ops:
  0.0 2.5 %copy-start = (bf16[128,1024]{1,0:T(8,128)(2,1)S(1)}, bf16[128,1024]{1,0:T(8,128)(2,1)}, u32[]{:S(2)}) copy-start(bf16[128,1024]{1,0:T(8,128)(2,1)} %param.14) | copy-start | bytes 786436
  0.0 26.4 %copy-start.4 = (f32[32,2]{0,1:T(2,128)S(1)}, f32[32,2]{0,1:T(2,128)}, u32[]{:S(2)}) copy-start(f32[32,2]{0,1:T(2,128)} %param.20) | copy-start | bytes 772
  0.0 26.4 %copy-start.5 = (s32[32,2]{0,1:T(2,128)S(1)}, s32[32,2]{0,1:T(2,128)}, u32[]{:S(2)}) copy-start(s32[32,2]{0,1:T(2,128)} %param.19) | copy-start | bytes 772
  0.0 32.5 %copy-start.2 = (f32[4096]{0:T(1024)S(1)}, f32[4096]{0:T(1024)}, u32[]{:S(2)}) copy-start(f32[4096]{0:T(1024)} %param.17) | copy-start | bytes 49156
  0.0 32.5 %copy-start.1 = (bf16[32,4096]{1,0:T(8,128)(2,1)S(1)}, bf16[32,4096]{1,0:T(8,128)(2,1)}, u32[]{:S(2)}) copy-start(bf16[32,4096]{1,0:T(8,128)(2,1)} %param.16) | copy-start | bytes 786436
  0.0 32.7 %copy-start.3 = (f32[4096]{0:T(1024)S(1)}, f32[4096]{0:T(1024)}, u32[]{:S(2)}) copy-start(f32[4096]{0:T(1024)} %param.18) | copy-start | bytes 49156
  23.0 9.4 %all-to-all-start = ((bf16[4,32,1024]{2,1,0:T(8,128)(2,1)}), bf16[4,32,1024]{2,1,0:T(8,128)(2,1)S(1)}, u32[]{:S(2)}, u32[]{:S(2)}) async-start(bf16[4,32,1024]{2,1,0:T(8,128)(2,1)} %all_to_all.10), calls=%async_computation | async-start | bytes 524288 | tf_op jit(solution)/shard_map/all_to_all | solution.py:556
  83.0 34.8 %slice-start = ((s8[9437184]{0:T(1024)(128)(4,1)}), s8[1048576]{0:T(1024)(128)(4,1)S(1)}, s32[]{:S(2)}) async-start(s8[9437184]{0:T(1024)(128)(4,1)} %bitcast.78), calls=%async_computation.1 | async-start | bytes 2097152
  83.0 34.8 %slice-start.1 = ((s8[9437184]{0:T(1024)(128)(4,1)}), s8[4194304]{0:T(1024)(128)(4,1)S(1)}, s32[]{:S(2)}) async-start(s8[9437184]{0:T(1024)(128)(4,1)} %bitcast.78), calls=%async_computation.2 | async-start | bytes 8388608
  100.8 17.1 %slice-start.2 = ((s8[9437184]{0:T(1024)(128)(4,1)}), s8[4194304]{0:T(1024)(128)(4,1)S(1)}, s32[]{:S(2)}) async-start(s8[9437184]{0:T(1024)(128)(4,1)} %bitcast.78), calls=%async_computation.3 | async-start | bytes 8388608
